TPU v7x, 256 devices: a whole 4x4x8 slice. The times are simulated.
256 devices in a mesh: rows: 16 (over z, core), feat: 16 (over x, y).
Axes of the slice: x: 4, y: 4, z: 8, core: 2. Of those that a mesh axis runs over, the one named last changes fastest.
Arguments:
- features: bfloat16 [16384, 16384], P('rows', 'feat'), may hold values from -0.046875 to 0.046875
- inverse_gram: float32 [16384, 1024], P('feat'), as said below
- targets: float32 [128, 16384], P('feat', 'rows'), may hold values from -6 to 6
Outputs:
- weights: float32 [128, 16384], P(None, 'feat')
- residual: float32 [128, 16384], P('feat', 'rows')
Inputs may be any that keep to these rules, and one draw needn't show every extreme that they name: Each block of inverse_gram is symmetric.
All inputs are finite; a program needn't handle non-finite values.
Results may differ from a plain program's by a relative error of at most 0.007.
Values sent between devices are 32-bit elements; how exact they have to be, the bound alone decides.
No kernel may reach another device: no remote copies, remote signals or barrier semaphores. Data moves between devices by JAX's collectives and lax.ppermute only.
A program may use at most 64 MiB of HBM per device.

v0:
```python
import jax
import jax.numpy as jnp
from jax import lax
from jax.sharding import PartitionSpec as P

TGT = 128
TURNS = 2
ridge_weight = 0.5


def passed_along(block, axis, distance):
    devices = range(lax.axis_size(axis))
    route = [((i - distance) % len(devices), i) for i in devices]
    return lax.ppermute(block, axis, route)


def local(features, inverse_gram, targets):
    block_count = lax.axis_size("feat")
    position = lax.axis_index("feat")
    panel_width = targets.shape[0]

    def refine(panel_rows, panel_weights):
        partial_value = jnp.dot(
            panel_rows.astype(jnp.bfloat16), features, preferred_element_type=jnp.float32
        )
        projection = lax.psum(partial_value, "rows")
        increment = jnp.dot(
            projection - ridge_weight * panel_weights, inverse_gram, precision=lax.Precision.HIGHEST
        )
        fitted = lax.dot_general(
            increment.astype(jnp.bfloat16),
            features,
            (((1,), (1,)), ((), ())),
            preferred_element_type=jnp.float32,
        )
        return (panel_rows - fitted, panel_weights + increment)

    def advance(section, carried):
        residual, weights = carried
        panel_index = (position - section) % block_count
        start = panel_index * panel_width
        panel_weights = lax.dynamic_slice_in_dim(weights, start, panel_width, 0)
        residual, panel_weights = refine(residual, panel_weights)
        weights = lax.dynamic_update_slice_in_dim(weights, panel_weights, start, 0)
        residual = passed_along(residual, "feat", 1)
        return (residual, weights)

    carried = (targets, jnp.zeros((TGT, features.shape[1]), jnp.float32))
    for sweep_index in range(TURNS):
        offset = sweep_index * block_count

        def sweep_step(inner, state, offset=offset):
            return advance(inner + offset, state)

        carried = lax.fori_loop(0, block_count, sweep_step, carried)
    residual, weights = carried
    return (weights, residual)


def solution(mesh):
    placed = (P("rows", "feat"), P("feat", None), P("feat", "rows"))
    return jax.shard_map(
        local,
        mesh=mesh,
        in_specs=placed,
        out_specs=(P(None, "feat"), P("feat", "rows")),
        check_vma=False,
    )
```

profile of v0, /device:TPU:0, one launch (start us, length us, event | category | flops | bytes accessed | tf_op | source)
XLA Modules:
  0.0 1925.4 jit_solution(16532286769631520528)
XLA Ops:
  1.4 963.3 %while.34 = (s32[]{:T(128)}, f32[8,1024]{1,0:T(8,128)S(1)}, f32[128,1024]{1,0:T(8,128)S(1)}, bf16[1024,1024]{1,0:T(8,128)(2,1)}, s32[]{:T(128)}, /*index=5*/f32[...) while((s32[]{:T(128)}, f32[8,1024]{1,0:T(8,128)S(1)}, ...), condition=%wide.region_2.3_spmd, body=%wide.region_0.2_spmd.sunk | while | flops 134275072 | bytes 17334632 | solution.py:55
  3.4 49.1 %psum.30 = f32[8,1024]{1,0:T(8,128)S(1)} all-reduce(f32[8,1024]{1,0:T(8,128)S(1)} %fusion.48), channel_id=1, replica_groups=mesh['rows'=16,'feat'=16] {'rows'}, use_global_device_ids=true, to_apply=%region_1.1 | all-reduce | flops 8192 | bytes 65536 | tf_op jit(solution)/shard_map/while/body/eval_jaxpr/psum | solution.py:26
  66.9 45.7 %psum.30 = f32[8,1024]{1,0:T(8,128)S(1)} all-reduce(f32[8,1024]{1,0:T(8,128)S(1)} %fusion.48), channel_id=1, replica_groups=mesh['rows'=16,'feat'=16] {'rows'}, use_global_device_ids=true, to_apply=%region_1.1 | all-reduce | flops 8192 | bytes 65536 | tf_op jit(solution)/shard_map/while/body/eval_jaxpr/psum | solution.py:26
  126.9 45.7 %psum.30 = f32[8,1024]{1,0:T(8,128)S(1)} all-reduce(f32[8,1024]{1,0:T(8,128)S(1)} %fusion.48), channel_id=1, replica_groups=mesh['rows'=16,'feat'=16] {'rows'}, use_global_device_ids=true, to_apply=%region_1.1 | all-reduce | flops 8192 | bytes 65536 | tf_op jit(solution)/shard_map/while/body/eval_jaxpr/psum | solution.py:26
  186.9 45.7 %psum.30 = f32[8,1024]{1,0:T(8,128)S(1)} all-reduce(f32[8,1024]{1,0:T(8,128)S(1)} %fusion.48), channel_id=1, replica_groups=mesh['rows'=16,'feat'=16] {'rows'}, use_global_device_ids=true, to_apply=%region_1.1 | all-reduce | flops 8192 | bytes 65536 | tf_op jit(solution)/shard_map/while/body/eval_jaxpr/psum | solution.py:26
  246.9 45.7 %psum.30 = f32[8,1024]{1,0:T(8,128)S(1)} all-reduce(f32[8,1024]{1,0:T(8,128)S(1)} %fusion.48), channel_id=1, replica_groups=mesh['rows'=16,'feat'=16] {'rows'}, use_global_device_ids=true, to_apply=%region_1.1 | all-reduce | flops 8192 | bytes 65536 | tf_op jit(solution)/shard_map/while/body/eval_jaxpr/psum | solution.py:26
  306.8 45.7 %psum.30 = f32[8,1024]{1,0:T(8,128)S(1)} all-reduce(f32[8,1024]{1,0:T(8,128)S(1)} %fusion.48), channel_id=1, replica_groups=mesh['rows'=16,'feat'=16] {'rows'}, use_global_device_ids=true, to_apply=%region_1.1 | all-reduce | flops 8192 | bytes 65536 | tf_op jit(solution)/shard_map/while/body/eval_jaxpr/psum | solution.py:26
  366.8 45.7 %psum.30 = f32[8,1024]{1,0:T(8,128)S(1)} all-reduce(f32[8,1024]{1,0:T(8,128)S(1)} %fusion.48), channel_id=1, replica_groups=mesh['rows'=16,'feat'=16] {'rows'}, use_global_device_ids=true, to_apply=%region_1.1 | all-reduce | flops 8192 | bytes 65536 | tf_op jit(solution)/shard_map/while/body/eval_jaxpr/psum | solution.py:26
  426.8 45.7 %psum.30 = f32[8,1024]{1,0:T(8,128)S(1)} all-reduce(f32[8,1024]{1,0:T(8,128)S(1)} %fusion.48), channel_id=1, replica_groups=mesh['rows'=16,'feat'=16] {'rows'}, use_global_device_ids=true, to_apply=%region_1.1 | all-reduce | flops 8192 | bytes 65536 | tf_op jit(solution)/shard_map/while/body/eval_jaxpr/psum | solution.py:26
  486.8 45.7 %psum.30 = f32[8,1024]{1,0:T(8,128)S(1)} all-reduce(f32[8,1024]{1,0:T(8,128)S(1)} %fusion.48), channel_id=1, replica_groups=mesh['rows'=16,'feat'=16] {'rows'}, use_global_device_ids=true, to_apply=%region_1.1 | all-reduce | flops 8192 | bytes 65536 | tf_op jit(solution)/shard_map/while/body/eval_jaxpr/psum | solution.py:26
  546.8 45.7 %psum.30 = f32[8,1024]{1,0:T(8,128)S(1)} all-reduce(f32[8,1024]{1,0:T(8,128)S(1)} %fusion.48), channel_id=1, replica_groups=mesh['rows'=16,'feat'=16] {'rows'}, use_global_device_ids=true, to_apply=%region_1.1 | all-reduce | flops 8192 | bytes 65536 | tf_op jit(solution)/shard_map/while/body/eval_jaxpr/psum | solution.py:26
  606.8 45.7 %psum.30 = f32[8,1024]{1,0:T(8,128)S(1)} all-reduce(f32[8,1024]{1,0:T(8,128)S(1)} %fusion.48), channel_id=1, replica_groups=mesh['rows'=16,'feat'=16] {'rows'}, use_global_device_ids=true, to_apply=%region_1.1 | all-reduce | flops 8192 | bytes 65536 | tf_op jit(solution)/shard_map/while/body/eval_jaxpr/psum | solution.py:26
  666.8 45.7 %psum.30 = f32[8,1024]{1,0:T(8,128)S(1)} all-reduce(f32[8,1024]{1,0:T(8,128)S(1)} %fusion.48), channel_id=1, replica_groups=mesh['rows'=16,'feat'=16] {'rows'}, use_global_device_ids=true, to_apply=%region_1.1 | all-reduce | flops 8192 | bytes 65536 | tf_op jit(solution)/shard_map/while/body/eval_jaxpr/psum | solution.py:26
  726.8 45.7 %psum.30 = f32[8,1024]{1,0:T(8,128)S(1)} all-reduce(f32[8,1024]{1,0:T(8,128)S(1)} %fusion.48), channel_id=1, replica_groups=mesh['rows'=16,'feat'=16] {'rows'}, use_global_device_ids=true, to_apply=%region_1.1 | all-reduce | flops 8192 | bytes 65536 | tf_op jit(solution)/shard_map/while/body/eval_jaxpr/psum | solution.py:26
  786.8 45.7 %psum.30 = f32[8,1024]{1,0:T(8,128)S(1)} all-reduce(f32[8,1024]{1,0:T(8,128)S(1)} %fusion.48), channel_id=1, replica_groups=mesh['rows'=16,'feat'=16] {'rows'}, use_global_device_ids=true, to_apply=%region_1.1 | all-reduce | flops 8192 | bytes 65536 | tf_op jit(solution)/shard_map/while/body/eval_jaxpr/psum | solution.py:26
  846.7 45.7 %psum.30 = f32[8,1024]{1,0:T(8,128)S(1)} all-reduce(f32[8,1024]{1,0:T(8,128)S(1)} %fusion.48), channel_id=1, replica_groups=mesh['rows'=16,'feat'=16] {'rows'}, use_global_device_ids=true, to_apply=%region_1.1 | all-reduce | flops 8192 | bytes 65536 | tf_op jit(solution)/shard_map/while/body/eval_jaxpr/psum | solution.py:26
  906.7 45.7 %psum.30 = f32[8,1024]{1,0:T(8,128)S(1)} all-reduce(f32[8,1024]{1,0:T(8,128)S(1)} %fusion.48), channel_id=1, replica_groups=mesh['rows'=16,'feat'=16] {'rows'}, use_global_device_ids=true, to_apply=%region_1.1 | all-reduce | flops 8192 | bytes 65536 | tf_op jit(solution)/shard_map/while/body/eval_jaxpr/psum | solution.py:26
  964.8 959.8 %while.35 = (s32[]{:T(128)}, f32[8,1024]{1,0:T(8,128)S(1)}, f32[128,1024]{1,0:T(8,128)S(1)}, bf16[1024,1024]{1,0:T(8,128)(2,1)}, s32[]{:T(128)}, /*index=5*/f32[...) while((s32[]{:T(128)}, f32[8,1024]{1,0:T(8,128)S(1)}, ...), condition=%wide.region_5.6_spmd, body=%wide.region_3.5_spmd.sunk | while | flops 134275072 | bytes 17334644 | solution.py:55
  966.7 45.7 %psum.31 = f32[8,1024]{1,0:T(8,128)S(1)} all-reduce(f32[8,1024]{1,0:T(8,128)S(1)} %fusion.56), channel_id=1, replica_groups=mesh['rows'=16,'feat'=16] {'rows'}, use_global_device_ids=true, to_apply=%region_4.4 | all-reduce | flops 8192 | bytes 65536 | tf_op jit(solution)/shard_map/while/body/eval_jaxpr/psum | solution.py:26
  1026.7 45.7 %psum.31 = f32[8,1024]{1,0:T(8,128)S(1)} all-reduce(f32[8,1024]{1,0:T(8,128)S(1)} %fusion.56), channel_id=1, replica_groups=mesh['rows'=16,'feat'=16] {'rows'}, use_global_device_ids=true, to_apply=%region_4.4 | all-reduce | flops 8192 | bytes 65536 | tf_op jit(solution)/shard_map/while/body/eval_jaxpr/psum | solution.py:26
  1086.7 45.7 %psum.31 = f32[8,1024]{1,0:T(8,128)S(1)} all-reduce(f32[8,1024]{1,0:T(8,128)S(1)} %fusion.56), channel_id=1, replica_groups=mesh['rows'=16,'feat'=16] {'rows'}, use_global_device_ids=true, to_apply=%region_4.4 | all-reduce | flops 8192 | bytes 65536 | tf_op jit(solution)/shard_map/while/body/eval_jaxpr/psum | solution.py:26
  1146.7 45.7 %psum.31 = f32[8,1024]{1,0:T(8,128)S(1)} all-reduce(f32[8,1024]{1,0:T(8,128)S(1)} %fusion.56), channel_id=1, replica_groups=mesh['rows'=16,'feat'=16] {'rows'}, use_global_device_ids=true, to_apply=%region_4.4 | all-reduce | flops 8192 | bytes 65536 | tf_op jit(solution)/shard_map/while/body/eval_jaxpr/psum | solution.py:26
  1206.7 45.7 %psum.31 = f32[8,1024]{1,0:T(8,128)S(1)} all-reduce(f32[8,1024]{1,0:T(8,128)S(1)} %fusion.56), channel_id=1, replica_groups=mesh['rows'=16,'feat'=16] {'rows'}, use_global_device_ids=true, to_apply=%region_4.4 | all-reduce | flops 8192 | bytes 65536 | tf_op jit(solution)/shard_map/while/body/eval_jaxpr/psum | solution.py:26
  1266.7 45.7 %psum.31 = f32[8,1024]{1,0:T(8,128)S(1)} all-reduce(f32[8,1024]{1,0:T(8,128)S(1)} %fusion.56), channel_id=1, replica_groups=mesh['rows'=16,'feat'=16] {'rows'}, use_global_device_ids=true, to_apply=%region_4.4 | all-reduce | flops 8192 | bytes 65536 | tf_op jit(solution)/shard_map/while/body/eval_jaxpr/psum | solution.py:26
  1326.7 45.7 %psum.31 = f32[8,1024]{1,0:T(8,128)S(1)} all-reduce(f32[8,1024]{1,0:T(8,128)S(1)} %fusion.56), channel_id=1, replica_groups=mesh['rows'=16,'feat'=16] {'rows'}, use_global_device_ids=true, to_apply=%region_4.4 | all-reduce | flops 8192 | bytes 65536 | tf_op jit(solution)/shard_map/while/body/eval_jaxpr/psum | solution.py:26
  1386.7 45.7 %psum.31 = f32[8,1024]{1,0:T(8,128)S(1)} all-reduce(f32[8,1024]{1,0:T(8,128)S(1)} %fusion.56), channel_id=1, replica_groups=mesh['rows'=16,'feat'=16] {'rows'}, use_global_device_ids=true, to_apply=%region_4.4 | all-reduce | flops 8192 | bytes 65536 | tf_op jit(solution)/shard_map/while/body/eval_jaxpr/psum | solution.py:26
  1446.6 45.7 %psum.31 = f32[8,1024]{1,0:T(8,128)S(1)} all-reduce(f32[8,1024]{1,0:T(8,128)S(1)} %fusion.56), channel_id=1, replica_groups=mesh['rows'=16,'feat'=16] {'rows'}, use_global_device_ids=true, to_apply=%region_4.4 | all-reduce | flops 8192 | bytes 65536 | tf_op jit(solution)/shard_map/while/body/eval_jaxpr/psum | solution.py:26
  1506.6 45.7 %psum.31 = f32[8,1024]{1,0:T(8,128)S(1)} all-reduce(f32[8,1024]{1,0:T(8,128)S(1)} %fusion.56), channel_id=1, replica_groups=mesh['rows'=16,'feat'=16] {'rows'}, use_global_device_ids=true, to_apply=%region_4.4 | all-reduce | flops 8192 | bytes 65536 | tf_op jit(solution)/shard_map/while/body/eval_jaxpr/psum | solution.py:26
  1566.6 45.7 %psum.31 = f32[8,1024]{1,0:T(8,128)S(1)} all-reduce(f32[8,1024]{1,0:T(8,128)S(1)} %fusion.56), channel_id=1, replica_groups=mesh['rows'=16,'feat'=16] {'rows'}, use_global_device_ids=true, to_apply=%region_4.4 | all-reduce | flops 8192 | bytes 65536 | tf_op jit(solution)/shard_map/while/body/eval_jaxpr/psum | solution.py:26
  1626.6 45.7 %psum.31 = f32[8,1024]{1,0:T(8,128)S(1)} all-reduce(f32[8,1024]{1,0:T(8,128)S(1)} %fusion.56), channel_id=1, replica_groups=mesh['rows'=16,'feat'=16] {'rows'}, use_global_device_ids=true, to_apply=%region_4.4 | all-reduce | flops 8192 | bytes 65536 | tf_op jit(solution)/shard_map/while/body/eval_jaxpr/psum | solution.py:26
  1686.6 45.7 %psum.31 = f32[8,1024]{1,0:T(8,128)S(1)} all-reduce(f32[8,1024]{1,0:T(8,128)S(1)} %fusion.56), channel_id=1, replica_groups=mesh['rows'=16,'feat'=16] {'rows'}, use_global_device_ids=true, to_apply=%region_4.4 | all-reduce | flops 8192 | bytes 65536 | tf_op jit(solution)/shard_map/while/body/eval_jaxpr/psum | solution.py:26
  1866.6 45.7 %psum.31 = f32[8,1024]{1,0:T(8,128)S(1)} all-reduce(f32[8,1024]{1,0:T(8,128)S(1)} %fusion.56), channel_id=1, replica_groups=mesh['rows'=16,'feat'=16] {'rows'}, use_global_device_ids=true, to_apply=%region_4.4 | all-reduce | flops 8192 | bytes 65536 | tf_op jit(solution)/shard_map/while/body/eval_jaxpr/psum | solution.py:26
  (263 shorter events, 549.7 us)
Async XLA Ops:
  57.7 7.3 collective-permute-start
  117.7 7.3 collective-permute-start
  177.6 7.3 collective-permute-start
  237.6 7.3 collective-permute-start
  297.6 7.3 collective-permute-start
  357.6 7.3 collective-permute-start
  417.6 7.3 collective-permute-start
  477.6 7.3 collective-permute-start
  537.6 7.3 collective-permute-start
  597.6 7.3 collective-permute-start
  657.6 7.3 collective-permute-start
  717.5 7.3 collective-permute-start
  777.5 7.3 collective-permute-start
  837.5 7.3 collective-permute-start
  897.5 7.3 collective-permute-start
  957.5 7.3 collective-permute-start
  1017.5 7.3 collective-permute-start.1
  1077.5 7.3 collective-permute-start.1
  1137.5 7.3 collective-permute-start.1
  1197.5 7.3 collective-permute-start.1
  1257.5 7.3 collective-permute-start.1
  1317.4 7.3 collective-permute-start.1
  1377.4 7.3 collective-permute-start.1
  1437.4 7.3 collective-permute-start.1
  1497.4 7.3 collective-permute-start.1
  1557.4 7.3 collective-permute-start.1
  1617.4 7.3 collective-permute-start.1
  1677.4 7.3 collective-permute-start.1
  1737.4 7.3 collective-permute-start.1
  1797.4 7.3 collective-permute-start.1
  1857.3 7.3 collective-permute-start.1
  1917.3 7.3 collective-permute-start.1
  (33 other events, 142.2 us)
where the time goes:
time: 1930 us
  blocking collectives  1470 us (76%)
  waiting for transfers between devices  229 us (12%)
  matrix products  225 us (12%)
    psum x32, blocking collectives, refine(): projection = lax.psum(partial_value, 'rows')  1470 us
    ppermute x32, waiting for transfers between devices, passed_along(): return lax.ppermute(block, axis, route)  229 us
    dot_general x32, matrix products, refine(): jnp.dot(projection - ridge_weight * panel_weights, inverse_gram, precisio...  141 us
    dot_general x32, matrix products, refine(): jnp.dot(panel_rows.astype(jnp.bfloat16), features, preferred_element_type...  63.1 us
  transfers between devices with their start and end apart: 32, of which 32 were waited for; matrix products, arithmetic and copies ran while one was open for 0% of the time, Pallas kernels for 0%

commit v1 on v0

--- a/solution.py
+++ b/solution.py
@@ -6,6 +6,14 @@
 TGT = 128
 TURNS = 2
 ridge_weight = 0.5
+
+
+def add_in_pairs(x, name):
+    n_dev, result = (lax.axis_size(name), x)
+    for reach in [1 << k for k in range(n_dev.bit_length() - 1)]:
+        swap = [(i, i ^ reach) for i in range(n_dev)]
+        result = result + lax.ppermute(result, name, swap)
+    return result
 
 
 def passed_along(block, axis, distance):
@@ -23,7 +31,7 @@
         partial_value = jnp.dot(
             panel_rows.astype(jnp.bfloat16), features, preferred_element_type=jnp.float32
         )
-        projection = lax.psum(partial_value, "rows")
+        projection = add_in_pairs(partial_value, "rows")
         increment = jnp.dot(
             projection - ridge_weight * panel_weights, inverse_gram, precision=lax.Precision.HIGHEST
         )

time: 1930 us -> 1030 us (0.53)
  blocking collectives: 1470 us -> 0 us
  waiting for transfers between devices: 229 us -> 638 us
  starting transfers between devices: 1.67 us -> 162 us
    psum x32 -> x0, blocking collectives: 1470 us -> none  [refine(): projection = lax.psum(partial_value, 'rows')]
    ppermute x0 -> x128, waiting for transfers between devices: none -> 408 us  [add_in_pairs(): result = result + lax.ppermute(result, name, swap)]
    ppermute x0 -> x128, starting transfers between devices: none -> 161 us  [add_in_pairs(): result = result + lax.ppermute(result, name, swap)]
  transfers between devices with their start and end apart: 32 -> 160, of which waited for: 32 -> 160; matrix products, arithmetic and copies ran while one was open for 0% -> 0% of each run, Pallas kernels for 0% -> 0%
where the time goes in v1:
time: 1030 us
  waiting for transfers between devices  638 us (62%)
  matrix products  225 us (22%)
  starting transfers between devices  162 us (16%)
    ppermute x128, waiting for transfers between devices, add_in_pairs(): result = result + lax.ppermute(result, name, swap)  408 us
    ppermute x32, waiting for transfers between devices, passed_along(): return lax.ppermute(block, axis, route)  230 us
    ppermute x128, starting transfers between devices, add_in_pairs(): result = result + lax.ppermute(result, name, swap)  161 us
    dot_general x32, matrix products, refine(): jnp.dot(projection - ridge_weight * panel_weights, inverse_gram, precisio...  141 us
    dot_general x32, matrix products, refine(): jnp.dot(panel_rows.astype(jnp.bfloat16), features, preferred_element_type...  63.1 us
  transfers between devices with their start and end apart: 160, of which 160 were waited for; matrix products, arithmetic and copies ran while one was open for 0% of the time, Pallas kernels for 0%

profile of v1, /device:TPU:0, one launch (start us, length us, event | category | flops | bytes accessed | tf_op | source)
XLA Modules:
  0.0 1029.8 jit_solution(11042574814025562035)
XLA Ops:
  1.4 514.4 %while.34 = (s32[]{:T(128)}, f32[8,1024]{1,0:T(8,128)S(1)}, f32[128,1024]{1,0:T(8,128)S(1)}, bf16[1024,1024]{1,0:T(8,128)(2,1)}, s32[]{:T(128)}, /*index=5*/f32[...) while((s32[]{:T(128)}, f32[8,1024]{1,0:T(8,128)S(1)}, ...), condition=%wide.region_1.2_spmd, body=%wide.region_0.1_spmd.sunk | while | flops 134299648 | bytes 18121224 | solution.py:63
  59.0 7.2 collective-permute-done.4
  91.1 7.2 collective-permute-done.4
  123.2 7.2 collective-permute-done.4
  155.2 7.2 collective-permute-done.4
  187.3 7.2 collective-permute-done.4
  219.8 7.2 collective-permute-done.4
  252.1 7.2 collective-permute-done.4
  284.1 7.2 collective-permute-done.4
  316.2 7.2 collective-permute-done.4
  348.3 7.2 collective-permute-done.4
  380.3 7.2 collective-permute-done.4
  412.4 7.2 collective-permute-done.4
  444.5 7.2 collective-permute-done.4
  476.5 7.2 collective-permute-done.4
  508.6 7.2 collective-permute-done.4
  515.8 513.1 %while.35 = (s32[]{:T(128)}, f32[8,1024]{1,0:T(8,128)S(1)}, f32[128,1024]{1,0:T(8,128)S(1)}, bf16[1024,1024]{1,0:T(8,128)(2,1)}, s32[]{:T(128)}, /*index=5*/f32[...) while((s32[]{:T(128)}, f32[8,1024]{1,0:T(8,128)S(1)}, ...), condition=%wide.region_3.4_spmd, body=%wide.region_2.3_spmd.sunk | while | flops 134299648 | bytes 18121236 | solution.py:63
  540.7 7.2 collective-permute-done.9
  572.8 7.2 collective-permute-done.9
  604.8 7.2 collective-permute-done.9
  636.9 7.2 collective-permute-done.9
  669.0 7.2 collective-permute-done.9
  701.0 7.2 collective-permute-done.9
  733.1 7.2 collective-permute-done.9
  765.2 7.2 collective-permute-done.9
  797.2 7.2 collective-permute-done.9
  829.3 7.2 collective-permute-done.9
  861.4 7.2 collective-permute-done.9
  893.5 7.2 collective-permute-done.9
  925.5 7.2 collective-permute-done.9
  957.6 7.2 collective-permute-done.9
  989.7 7.2 collective-permute-done.9
  (583 shorter events, 811.7 us)
Async XLA Ops:
  13.7 7.8 collective-permute-start.3
  46.1 7.8 collective-permute-start.3
  78.2 7.8 collective-permute-start.3
  110.2 7.8 collective-permute-start.3
  142.3 7.8 collective-permute-start.3
  174.4 7.8 collective-permute-start.3
  206.5 8.2 collective-permute-start.3
  238.9 8.1 collective-permute-start.3
  271.2 7.8 collective-permute-start.3
  303.3 7.8 collective-permute-start.3
  335.4 7.8 collective-permute-start.3
  367.4 7.8 collective-permute-start.3
  399.5 7.8 collective-permute-start.3
  431.6 7.8 collective-permute-start.3
  463.6 7.8 collective-permute-start.3
  495.7 7.8 collective-permute-start.3
  527.8 7.8 collective-permute-start.8
  559.8 7.8 collective-permute-start.8
  591.9 7.8 collective-permute-start.8
  624.0 7.8 collective-permute-start.8
  656.1 7.8 collective-permute-start.8
  688.1 7.8 collective-permute-start.8
  720.2 7.8 collective-permute-start.8
  752.3 7.8 collective-permute-start.8
  784.3 7.8 collective-permute-start.8
  816.4 7.8 collective-permute-start.8
  848.5 7.8 collective-permute-start.8
  880.5 7.8 collective-permute-start.8
  912.6 7.8 collective-permute-start.8
  944.7 7.8 collective-permute-start.8
  976.7 7.8 collective-permute-start.8
  1008.8 7.8 collective-permute-start.8
  (161 other events, 693.0 us)
